TPU v7x, 32 devices: a whole 2x2x4 slice. The times are simulated.
32 devices in a mesh: groups: 2 (over y), node: 4 (over z), feat: 4 (over x, core).
Axes of the slice: x: 2, y: 2, z: 4, core: 2. Of those that a mesh axis runs over, the one named last changes fastest.
Arguments:
- features: bfloat16 [12288, 256], P(('groups', 'node'), 'feat'), parts along dimension 0, may hold values from -6 to 6
- tiles: bfloat16 [96, 8, 128, 128], P(('groups', 'node')), parts along dimension 0, may hold values from 0 to 0.0625
- col_block: int32 [96, 8], P(('groups', 'node')), parts along dimension 0, may hold values from 0 to 47, as said below
- weight: bfloat16 [256, 172], replicated, may hold values from -0.375 to 0.375
- bias: float32 [172], replicated, may hold values from -1 to 1
Outputs:
- logits: bfloat16 [12288, 172], P(('groups', 'node', 'feat')), parts along dimension 0
There are 2 independent parts, one for each index of `groups`. A program takes and returns all parts, laid end to end along the dimension named above; an argument that names none is the same for every part. Nothing has to cross between parts.
Inputs may be any that keep to these rules, and one draw needn't show every extreme that they name: `col_block`: stripe d holds block rows d * 12 to (d + 1) * 12 - 1. Slot 0 of block row r is r itself; every other slot names a block of another stripe. Over the block rows of one stripe, at most 28 slots name blocks of any one other stripe, and exactly 28 name blocks of some other stripe. The same block may be named more than once.
All inputs are finite; a program needn't handle non-finite values.
Results may differ from a plain program's by a relative error of at most 0.0046.
Values may be sent and summed in bfloat16 or wider, within the bound.
A program may use at most 128 MiB of HBM per device.

v0:
```python
import functools

import jax
import jax.numpy as jnp
from jax import lax
from jax.experimental import pallas as pl
from jax.experimental.pallas import tpu as pltpu
from jax.sharding import PartitionSpec as P

MESH = pl.DeviceIdType.MESH
PHASES = ((0, 1), (2, 3))
PIECES = 4


def kernel(nodes, feats, cols_hbm, x, tiles_hbm, weight_hbm, bias_hbm, out, cols, weight, bias, column, tiles, agg, parts,
           full, own_sem, tile_sem, small_sem, right_send, right_recv, left_send, left_recv, ex_send, ex_recv, *held):
    node = lax.axis_index("node")
    feat = lax.axis_index("feat")
    width = x.shape[0]
    piece = width // PIECES
    block_rows, slots, block, _ = tiles.shape
    share = block_rows // feats
    span = share * block

    def stripe_of(p, stripe):
        return held[p].at[pl.ds(stripe * block_rows, block_rows)]

    for p in range(PIECES):
        for b in range(block_rows):
            pltpu.make_async_copy(
                x.at[pl.ds(p * piece, piece), pl.ds(b * block, block)],
                held[p].at[node * block_rows + b],
                own_sem.at[p],
            ).start()
    barrier = pltpu.get_barrier_semaphore()

    @pl.when(node > 0)
    def _():
        pl.semaphore_signal(barrier, inc=1, device_id={"node": node - 1}, device_id_type=MESH)

    @pl.when(node < nodes - 1)
    def _():
        pl.semaphore_signal(barrier, inc=1, device_id={"node": node + 1}, device_id_type=MESH)

    for k in range(1, feats):
        pl.semaphore_signal(
            barrier, inc=1, device_id={"feat": lax.rem(feat + k, feats)}, device_id_type=MESH
        )
    neighbours = jnp.where(node > 0, 1, 0) + jnp.where(node < nodes - 1, 1, 0)
    pl.semaphore_wait(barrier, neighbours + (feats - 1))

    def right(step, p):
        stripe = jnp.maximum(node - step, 0)
        return pltpu.make_async_remote_copy(
            stripe_of(p, stripe), stripe_of(p, stripe), right_send.at[step, p], right_recv.at[step, p],
            device_id={"node": jnp.minimum(node + 1, nodes - 1)}, device_id_type=MESH,
        )

    def left(step, p):
        stripe = jnp.minimum(node + step, nodes - 1)
        return pltpu.make_async_remote_copy(
            stripe_of(p, stripe), stripe_of(p, stripe), left_send.at[step, p], left_recv.at[step, p],
            device_id={"node": jnp.maximum(node - 1, 0)}, device_id_type=MESH,
        )

    def sends_right(step):
        return jnp.logical_and(node < nodes - 1, node >= step)

    def sends_left(step):
        return jnp.logical_and(node > 0, node + step <= nodes - 1)

    def takes_left(step):
        return node + 1 + step <= nodes - 1

    def takes_right(step):
        return node - 1 - step >= 0

    def send(step, p):
        if step == 0:
            own = stripe_of(p, node)
            pltpu.make_async_copy(own, own, own_sem.at[p]).wait()
        pl.when(sends_right(step))(lambda: right(step, p).start())
        pl.when(sends_left(step))(lambda: left(step, p).start())

    def take(step, p):
        pl.when(takes_right(step))(lambda: right(step, p).wait_recv())
        pl.when(takes_left(step))(lambda: left(step, p).wait_recv())

    def forward_phase(pieces):
        for step in range(1, nodes - 1):
            for p in pieces:
                take(step - 1, p)
                send(step, p)

    def finish_phase(pieces):
        for p in pieces:
            take(nodes - 2, p)

    def exchange(phase, k):
        pieces = PHASES[phase]
        height = piece * len(pieces)
        low = pieces[0] * piece
        peer = lax.rem(feat + k, feats)
        return pltpu.make_async_remote_copy(
            agg.at[pl.ds(low, height), pl.ds(pl.multiple_of(peer * span, span), span)],
            full[phase].at[pl.ds(pl.multiple_of(feat * height, height), height)],
            ex_send.at[phase, k], ex_recv.at[phase, k],
            device_id={"feat": peer}, device_id_type=MESH,
        )

    order = list(range(1, feats))
    if feats == 4:
        odd = lax.rem(feat, 2)
        order = [2, 3 - 2 * odd, 1 + 2 * odd]

    def aggregate(phase):
        pieces = PHASES[phase]
        height = piece * len(pieces)
        low = pieces[0] * piece
        for k in order + [0]:
            peer = lax.rem(feat + k, feats)
            sums = []
            for j in range(share):
                r = peer * share + j
                picked = [
                    jnp.concatenate([held[p][cols[s, r]] for p in pieces], axis=0)
                    for s in range(slots)
                ]
                sums.append(lax.dot_general(
                    jnp.concatenate([tiles[r, s] for s in range(slots)], axis=1),
                    jnp.concatenate(picked, axis=1),
                    (((1,), (1,)), ((), ())),
                    preferred_element_type=jnp.float32,
                ))
            rounded = jnp.concatenate([part.T for part in sums], axis=1).astype(jnp.bfloat16)
            if isinstance(k, int) and k == 0:
                here = pl.ds(pl.multiple_of(feat * height, height), height)
                full[phase][here, :] = rounded
            else:
                there = pl.ds(pl.multiple_of(peer * span, span), span)
                agg[pl.ds(low, height), there] = rounded
            if not (isinstance(k, int) and k == 0):
                exchange(phase, k).start()

    def project(phase):
        for k in range(1, feats):
            exchange(phase, k).wait_recv()
        return jnp.dot(parts[phase], full[phase][...], preferred_element_type=jnp.float32)

    for p in range(PIECES):
        send(0, p)
    tile_copy = pltpu.make_async_copy(tiles_hbm, tiles, tile_sem)
    tile_copy.start()
    cols_copy = pltpu.make_async_copy(cols_hbm, cols, small_sem.at[0])
    cols_copy.start()
    weight_copy = pltpu.make_async_copy(weight_hbm, weight, small_sem.at[1])
    weight_copy.start()
    bias_copy = pltpu.make_async_copy(bias_hbm, bias, small_sem.at[2])
    bias_copy.start()

    forward_phase(range(PIECES))
    weight_copy.wait()
    for phase, pieces in enumerate(PHASES):
        low, high = pieces[0] * piece, (pieces[-1] + 1) * piece
        parts[phase] = jnp.concatenate(
            [weight[:, f * width + low : f * width + high] for f in range(feats)], axis=1
        )
    bias_copy.wait()
    column[...] = jnp.broadcast_to(bias[...], (block, bias.shape[1])).T
    cols_copy.wait()
    tile_copy.wait()
    for phase, pieces in enumerate(PHASES):
        finish_phase(pieces)
        aggregate(phase)

    total = jnp.concatenate([column[...]] * share, axis=1)
    for phase in range(len(PHASES)):
        total += project(phase)
    out[...] = total.astype(out.dtype)

    for step in range(nodes - 1):
        for p in range(PIECES):
            pl.when(sends_right(step))(lambda: right(step, p).wait_send())
            pl.when(sends_left(step))(lambda: left(step, p).wait_send())
    for phase in range(len(PHASES)):
        for k in range(1, feats):
            exchange(phase, k).wait_send()


def on_device(nodes, feats, features, tiles, col_block, weight, bias):
    rows, width = features.shape
    block_rows, slots, block, _ = tiles.shape
    share = rows // feats
    phases = len(PHASES)
    classes = weight.shape[1]
    half = feats * width // phases
    logits = pl.pallas_call(
        functools.partial(kernel, nodes, feats),
        out_shape=jax.ShapeDtypeStruct((classes, share), jnp.bfloat16),
        in_specs=[
            pl.BlockSpec(memory_space=pl.ANY),
            pl.BlockSpec(memory_space=pl.ANY),
            pl.BlockSpec(memory_space=pl.ANY),
            pl.BlockSpec(memory_space=pl.ANY),
            pl.BlockSpec(memory_space=pl.ANY),
        ],
        out_specs=pl.BlockSpec(memory_space=pltpu.VMEM),
        scratch_shapes=[
            pltpu.SMEM(col_block.shape[::-1], col_block.dtype),
            pltpu.VMEM(weight.shape[::-1], weight.dtype),
            pltpu.VMEM((1, classes), bias.dtype),
            pltpu.VMEM((classes, block), bias.dtype),
            pltpu.VMEM(tiles.shape, tiles.dtype),
            pltpu.VMEM((width, rows), features.dtype),
            pltpu.VMEM((phases, classes, half), weight.dtype),
            [pltpu.VMEM((half, share), features.dtype)] * phases,
            pltpu.SemaphoreType.DMA((PIECES,)),
            pltpu.SemaphoreType.DMA,
            pltpu.SemaphoreType.DMA((3,)),
            pltpu.SemaphoreType.DMA((nodes - 1, PIECES)),
            pltpu.SemaphoreType.DMA((nodes - 1, PIECES)),
            pltpu.SemaphoreType.DMA((nodes - 1, PIECES)),
            pltpu.SemaphoreType.DMA((nodes - 1, PIECES)),
            pltpu.SemaphoreType.DMA((phases, feats)),
            pltpu.SemaphoreType.DMA((phases, feats)),
            *[pltpu.VMEM((nodes * block_rows, width // PIECES, block), features.dtype)] * PIECES,
        ],
        compiler_params=pltpu.CompilerParams(collective_id=0, has_side_effects=True),
    )(col_block.T, features.T, tiles, weight.T, bias[None])
    return logits.T


def solution(mesh):
    in_specs = (
        P(("groups", "node"), "feat"),
        P(("groups", "node"), None, None, None),
        P(("groups", "node"), None),
        P(),
        P(),
    )
    out_specs = P(("groups", "node", "feat"), None)
    body = functools.partial(on_device, mesh.shape["node"], mesh.shape["feat"])
    return jax.shard_map(
        body, mesh=mesh, in_specs=in_specs, out_specs=out_specs, check_vma=False
    )
```

profile of v0, /device:TPU:0, one launch (start us, length us, event | category | flops | bytes accessed | tf_op | source)
XLA Modules:
  0.0 25.4 jit_solution(9930628497479800159)
XLA Ops:
  0.0 23.8 %shard_map.55 = bf16[172,384]{1,0:T(8,128)(2,1)} custom-call(s32[8,12]{1,0:T(8,128)} %bitcast.8, bf16[64,1536]{1,0:T(8,128)(2,1)} %bitcast.6, bf16[12,8,128,128]{3,2,1,0:T(8,128)(2,1)} %tiles_hbm.1, bf16[172,256]{1,0:T(8,128)(2,1)} %bitcast.7, f32[1,172]{1,0:T(1,128)} %bitcast.9), custom_call_target="tpu_custom_call" | custom-call | tf_op jit(solution)/shard_map/pallas_call | solution.py:197
  23.8 1.6 %copy.7 = bf16[384,172]{0,1:T(8,128)(2,1)} copy(bf16[384,172]{0,1:T(8,128)(2,1)} %bitcast.5) | data formatting | bytes 264192
where the time goes:
time: 25.5 us; the launch traced here: 25.4 us
  Pallas kernels  23.8 us (93%)
  local copies, waits for them, and re-layouts  1.58 us (6%)
    pallas_call x1, Pallas kernels, on_device(): pl.pallas_call(functools.partial(kernel, nodes, feats), out_shape=jax.Sha...  23.8 us
    unnamed x1, local copies, waits for them, and re-layouts  1.58 us

commit v1 on v0

--- a/solution.py
+++ b/solution.py
@@ -196,7 +196,7 @@
     half = feats * width // phases
     logits = pl.pallas_call(
         functools.partial(kernel, nodes, feats),
-        out_shape=jax.ShapeDtypeStruct((classes, share), jnp.bfloat16),
+        out_shape=pltpu.VMEM((classes, share), jnp.bfloat16),
         in_specs=[
             pl.BlockSpec(memory_space=pl.ANY),
             pl.BlockSpec(memory_space=pl.ANY),

time: 25.5 us -> 24 us (0.941)
  local copies, waits for them, and re-layouts: 1.58 us -> 0.66 us
  Pallas kernels: 23.8 us -> 23.2 us
    unnamed x1, local copies, waits for them, and re-layouts: 1.58 us -> 0.66 us
    pallas_call x1, Pallas kernels: 23.8 us -> 23.2 us  [on_device(): pl.pallas_call(functools.partial(kernel, nodes, feats), out_shape=pltpu.V...]
where the time goes in v1:
time: 24 us; the launch traced here: 23.8 us
  Pallas kernels  23.2 us (97%)
  local copies, waits for them, and re-layouts  0.66 us (3%)
    pallas_call x1, Pallas kernels, on_device(): pl.pallas_call(functools.partial(kernel, nodes, feats), out_shape=pltpu.V...  23.2 us
    unnamed x1, local copies, waits for them, and re-layouts  0.66 us

profile of v1, /device:TPU:0, one launch (start us, length us, event | category | flops | bytes accessed | tf_op | source)
XLA Modules:
  0.0 23.8 jit_solution(2946738082080191985)
XLA Ops:
  0.0 23.2 %shard_map.55 = bf16[172,384]{1,0:T(8,128)(2,1)S(1)} custom-call(s32[8,12]{1,0:T(8,128)} %bitcast.8, bf16[64,1536]{1,0:T(8,128)(2,1)} %bitcast.6, bf16[12,8,128,128]{3,2,1,0:T(8,128)(2,1)} %tiles_hbm.1, bf16[172,256]{1,0:T(8,128)(2,1)} %bitcast.7, f32[1,172]{1,0:T(1,128)} %bitcast.9), custom_call_target="tpu_custom_call" | custom-call | tf_op jit(solution)/shard_map/pallas_call | solution.py:197
  23.2 0.7 %copy.7 = bf16[384,172]{0,1:T(8,128)(2,1)} copy(bf16[384,172]{0,1:T(8,128)(2,1)S(1)} %bitcast.5) | data formatting | bytes 264192

commit v2 on v1

v2 whole, which is shorter than its diff:
```python
import functools

import jax
import jax.numpy as jnp
from jax import lax
from jax.experimental import pallas as pl
from jax.experimental.pallas import tpu as pltpu
from jax.sharding import PartitionSpec as P

MESH = pl.DeviceIdType.MESH
PIECES = 4


def kernel(nodes, feats, cols_hbm, x, tiles_hbm, weight_hbm, bias_hbm, out, cols, weight, bias, column, tiles, agg, full, blocks, own_sem, tile_sem, small_sem, right_send, right_recv, left_send, left_recv,
           ex_send, ex_recv, right_in, above_in, feats_in, *held):
    node = lax.axis_index("node")
    feat = lax.axis_index("feat")
    odd = lax.rem(feat, 2)
    width = x.shape[0]
    piece = width // PIECES
    block_rows, slots, block, _ = tiles.shape
    share = block_rows // feats
    span = share * block
    stripe_rows = block_rows * block
    peers = [lax.rem(feat + k, feats) for k in range(1, feats)]

    barrier = pltpu.get_barrier_semaphore()

    @pl.when(node < nodes - 1)
    def _():
        pl.semaphore_signal(barrier, inc=1, device_id={"node": node + 1}, device_id_type=MESH)

    @pl.when(node == 0)
    def _():
        for peer in peers:
            pl.semaphore_signal(barrier, inc=1, device_id={"feat": peer}, device_id_type=MESH)

    pl.semaphore_wait(barrier, jnp.where(node == 0, feats - 1, 1))

    @pl.when(node > 0)
    def _():
        pl.semaphore_signal(right_in, inc=1, device_id={"node": node - 1}, device_id_type=MESH)

    def meet():
        @pl.when(node > 0)
        def _():
            pl.semaphore_wait(feats_in, 1)

        @pl.when(node < nodes - 1)
        def _():
            for peer in peers:
                pl.semaphore_signal(above_in, inc=1, device_id={"feat": peer}, device_id_type=MESH)
            pl.semaphore_wait(above_in, feats - 1)
            pl.semaphore_signal(feats_in, inc=1, device_id={"node": node + 1}, device_id_type=MESH)

    def stripe_of(p, stripe):
        return held[p].at[:, pl.ds(pl.multiple_of(stripe * stripe_rows, stripe_rows), stripe_rows)]

    def source(step, p, stripe):
        return x.at[pl.ds(p * piece, piece)] if step == 0 else stripe_of(p, stripe)

    def right(step, p):
        stripe = jnp.maximum(node - step, 0)
        return pltpu.make_async_remote_copy(
            source(step, p, stripe), stripe_of(p, stripe), right_send.at[step, p], right_recv.at[step, p],
            device_id={"node": jnp.minimum(node + 1, nodes - 1)}, device_id_type=MESH,
        )

    def left(step, p):
        stripe = jnp.minimum(node + step, nodes - 1)
        return pltpu.make_async_remote_copy(
            source(step, p, stripe), stripe_of(p, stripe), left_send.at[step, p], left_recv.at[step, p],
            device_id={"node": jnp.maximum(node - 1, 0)}, device_id_type=MESH,
        )

    def sends_right(step):
        return jnp.logical_and(node < nodes - 1, node >= step)

    def sends_left(step):
        return jnp.logical_and(node > 0, node + step <= nodes - 1)

    def takes_left(step):
        return node + 1 + step <= nodes - 1

    def takes_right(step):
        return node - 1 - step >= 0

    def send(step, p):
        pl.when(sends_right(step))(lambda: right(step, p).start())
        pl.when(sends_left(step))(lambda: left(step, p).start())

    def take(step, p):
        pl.when(takes_right(step))(lambda: right(step, p).wait_recv())
        pl.when(takes_left(step))(lambda: left(step, p).wait_recv())

    def unpack_stripe(p, stripe):
        def one(b, carry):
            at = pl.multiple_of(stripe * stripe_rows + b * block, block)
            blocks[stripe * block_rows + b, p * piece:(p + 1) * piece, :] = held[p][:, pl.ds(at, block)]
            return carry

        lax.fori_loop(0, block_rows, one, 0, unroll=False)

    def unpack(step, p):
        pl.when(takes_right(step))(lambda: unpack_stripe(p, node - 1 - step))
        pl.when(takes_left(step))(lambda: unpack_stripe(p, node + 1 + step))

    order = list(range(1, feats))
    if feats == 4:
        order = [2 - odd, 3 - odd, 1 + 2 * odd]

    def exchange(k):
        peer = lax.rem(feat + k, feats)
        return pltpu.make_async_remote_copy(
            agg.at[:, pl.ds(pl.multiple_of(peer * span, span), span)],
            full.at[pl.ds(pl.multiple_of(feat * width, width), width)],
            ex_send.at[k], ex_recv.at[k], device_id={"feat": peer}, device_id_type=MESH,
        )

    def aggregate(i, carry):
        k = jnp.int32(0)
        for at, step in enumerate(order):
            k = jnp.where(i == at, step, k)
        peer = lax.rem(feat + k, feats)
        sums = []
        for j in range(share):
            r = peer * share + j
            sums.append(lax.dot_general(
                jnp.concatenate([blocks[cols[s, r]] for s in range(slots)], axis=1),
                jnp.concatenate([tiles[r, s] for s in range(slots)], axis=1),
                (((1,), (1,)), ((), ())),
                preferred_element_type=jnp.float32,
            ))
        rounded = jnp.concatenate(sums, axis=1).astype(jnp.bfloat16)
        agg[:, pl.ds(pl.multiple_of(peer * span, span), span)] = rounded

        @pl.when(i < feats - 1)
        def _():
            exchange(k).start()

        return carry

    for p in range(PIECES):
        pl.when(sends_left(0))(lambda: left(0, p).start())

    @pl.when(node < nodes - 1)
    def _():
        pl.semaphore_wait(right_in, 1)

    for p in range(PIECES):
        pl.when(sends_right(0))(lambda: right(0, p).start())
    own = [pltpu.make_async_copy(source(0, p, node), stripe_of(p, node), own_sem.at[p]) for p in range(PIECES)]
    for copy in own:
        copy.start()
    weight_copy = pltpu.make_async_copy(weight_hbm, weight, small_sem.at[1])
    weight_copy.start()
    bias_copy = pltpu.make_async_copy(bias_hbm, bias, small_sem.at[2])
    bias_copy.start()
    cols_copy = pltpu.make_async_copy(cols_hbm, cols, small_sem.at[0])
    cols_copy.start()
    tile_copy = pltpu.make_async_copy(tiles_hbm, tiles, tile_sem)
    tile_copy.start()

    pl.when(node <= 1)(meet)
    weight_copy.wait()
    bias_copy.wait()
    column[...] = jnp.broadcast_to(bias[...], (block, bias.shape[1])).T
    for step in range(1, nodes - 1):
        for p in range(PIECES):
            take(step - 1, p)
            send(step, p)
    pl.when(node > 1)(meet)
    for p in range(PIECES):
        own[p].wait()
        unpack_stripe(p, node)
    for step in range(nodes - 2):
        for p in range(PIECES):
            unpack(step, p)
    cols_copy.wait()
    tile_copy.wait()
    for p in range(PIECES):
        take(nodes - 2, p)
        unpack(nodes - 2, p)

    lax.fori_loop(0, feats, aggregate, 0)

    here = pl.ds(pl.multiple_of(feat * span, span), span)
    full[pl.ds(pl.multiple_of(feat * width, width), width), :] = agg[:, here]

    total = jnp.concatenate([column[...]] * share, axis=1)
    for k in range(1, feats):
        exchange(k).wait_recv()
    total += jnp.dot(weight[...], full[...], preferred_element_type=jnp.float32)
    out[...] = total.astype(out.dtype)

    for step in range(nodes - 1):
        for p in range(PIECES):
            pl.when(sends_right(step))(lambda: right(step, p).wait_send())
            pl.when(sends_left(step))(lambda: left(step, p).wait_send())
    for k in range(1, feats):
        exchange(k).wait_send()


def on_device(nodes, feats, features, tiles, col_block, weight, bias):
    rows, width = features.shape
    block_rows, _, block, _ = tiles.shape
    share = rows // feats
    classes = weight.shape[1]
    piece = width // PIECES
    logits = pl.pallas_call(
        functools.partial(kernel, nodes, feats),
        out_shape=pltpu.VMEM((classes, share), jnp.bfloat16),
        in_specs=[
            pl.BlockSpec(memory_space=pl.ANY),
            pl.BlockSpec(memory_space=pl.ANY),
            pl.BlockSpec(memory_space=pl.ANY),
            pl.BlockSpec(memory_space=pl.ANY),
            pl.BlockSpec(memory_space=pl.ANY),
        ],
        out_specs=pl.BlockSpec(memory_space=pltpu.VMEM),
        scratch_shapes=[
            pltpu.SMEM(col_block.shape[::-1], col_block.dtype),
            pltpu.VMEM(weight.shape[::-1], weight.dtype),
            pltpu.VMEM((1, classes), bias.dtype),
            pltpu.VMEM((classes, block), bias.dtype),
            pltpu.VMEM(tiles.shape, tiles.dtype),
            pltpu.VMEM((width, rows), features.dtype),
            pltpu.VMEM((feats * width, share), features.dtype),
            pltpu.VMEM((nodes * block_rows, width, block), features.dtype),
            pltpu.SemaphoreType.DMA((PIECES,)),
            pltpu.SemaphoreType.DMA,
            pltpu.SemaphoreType.DMA((3,)),
            pltpu.SemaphoreType.DMA((nodes - 1, PIECES)),
            pltpu.SemaphoreType.DMA((nodes - 1, PIECES)),
            pltpu.SemaphoreType.DMA((nodes - 1, PIECES)),
            pltpu.SemaphoreType.DMA((nodes - 1, PIECES)),
            pltpu.SemaphoreType.DMA((feats,)),
            pltpu.SemaphoreType.DMA((feats,)),
            pltpu.SemaphoreType.REGULAR,
            pltpu.SemaphoreType.REGULAR,
            pltpu.SemaphoreType.REGULAR,
            *[pltpu.VMEM((piece, nodes * rows), features.dtype)] * PIECES,
        ],
        compiler_params=pltpu.CompilerParams(collective_id=0, has_side_effects=True),
    )(col_block.T, features.T, tiles, weight.T, bias[None])
    return logits.T


def solution(mesh):
    in_specs = (
        P(("groups", "node"), "feat"),
        P(("groups", "node"), None, None, None),
        P(("groups", "node"), None),
        P(),
        P(),
    )
    out_specs = P(("groups", "node", "feat"), None)
    body = functools.partial(on_device, mesh.shape["node"], mesh.shape["feat"])
    return jax.shard_map(
        body, mesh=mesh, in_specs=in_specs, out_specs=out_specs, check_vma=False
    )
```

time: 24 us -> 22.7 us (0.946)
  Pallas kernels: 23.2 us -> 21.9 us
    pallas_call x1, Pallas kernels: 23.2 us -> 21.9 us  [on_device(): pl.pallas_call(functools.partial(kernel, nodes, feats), out_shape=pltpu.V...]
where the time goes in v2:
time: 22.7 us; the launch traced here: 22.6 us
  Pallas kernels  21.9 us (96%)
  local copies, waits for them, and re-layouts  0.66 us (3%)
    pallas_call x1, Pallas kernels, on_device(): pl.pallas_call(functools.partial(kernel, nodes, feats), out_shape=pltpu.V...  21.9 us
    unnamed x1, local copies, waits for them, and re-layouts  0.66 us

profile of v2, /device:TPU:0, one launch (start us, length us, event | category | flops | bytes accessed | tf_op | source)
XLA Modules:
  0.0 22.6 jit_solution(4983983997554572935)
XLA Ops:
  0.0 21.9 %shard_map.55 = bf16[172,384]{1,0:T(8,128)(2,1)S(1)} custom-call(s32[8,12]{1,0:T(8,128)} %bitcast.8, bf16[64,1536]{1,0:T(8,128)(2,1)} %bitcast.6, bf16[12,8,128,128]{3,2,1,0:T(8,128)(2,1)} %tiles_hbm.1, bf16[172,256]{1,0:T(8,128)(2,1)} %bitcast.7, f32[1,172]{1,0:T(1,128)} %bitcast.9), custom_call_target="tpu_custom_call" | custom-call | tf_op jit(solution)/shard_map/pallas_call | solution.py:210
  21.9 0.7 %copy.7 = bf16[384,172]{0,1:T(8,128)(2,1)} copy(bf16[384,172]{0,1:T(8,128)(2,1)S(1)} %bitcast.5) | data formatting | bytes 264192

commit v3 on v2

--- a/solution.py
+++ b/solution.py
@@ -9,6 +9,7 @@
 
 MESH = pl.DeviceIdType.MESH
 PIECES = 4
+LAG = 0
 
 
 def kernel(nodes, feats, cols_hbm, x, tiles_hbm, weight_hbm, bias_hbm, out, cols, weight, bias, column, tiles, agg, full, blocks, own_sem, tile_sem, small_sem, right_send, right_recv, left_send, left_recv,
@@ -84,10 +85,6 @@
 
     def takes_right(step):
         return node - 1 - step >= 0
-
-    def send(step, p):
-        pl.when(sends_right(step))(lambda: right(step, p).start())
-        pl.when(sends_left(step))(lambda: left(step, p).start())
 
     def take(step, p):
         pl.when(takes_right(step))(lambda: right(step, p).wait_recv())
@@ -140,15 +137,18 @@
 
         return carry
 
-    for p in range(PIECES):
-        pl.when(sends_left(0))(lambda: left(0, p).start())
+    @pl.when(sends_left(0))
+    def _():
+        for p in range(PIECES):
+            left(0, p).start()
+
 
     @pl.when(node < nodes - 1)
     def _():
         pl.semaphore_wait(right_in, 1)
-
-    for p in range(PIECES):
-        pl.when(sends_right(0))(lambda: right(0, p).start())
+        for p in range(PIECES):
+            right(0, p).start()
+
     own = [pltpu.make_async_copy(source(0, p, node), stripe_of(p, node), own_sem.at[p]) for p in range(PIECES)]
     for copy in own:
         copy.start()
@@ -161,21 +161,31 @@
     tile_copy = pltpu.make_async_copy(tiles_hbm, tiles, tile_sem)
     tile_copy.start()
 
-    pl.when(node <= 1)(meet)
+    pl.when(node == 0)(meet)
+    turns = [(step, p) for step in range(1, nodes - 1) for p in range(PIECES)]
+    for at in range(len(turns) + LAG):
+        if at < len(turns):
+            step, p = turns[at]
+            pl.when(takes_left(step - 1))(lambda: left(step - 1, p).wait_recv())
+            pl.when(sends_left(step))(lambda: left(step, p).start())
+        if at >= LAG:
+            step, p = turns[at - LAG]
+            pl.when(takes_right(step - 1))(lambda: right(step - 1, p).wait_recv())
+            pl.when(sends_right(step))(lambda: right(step, p).start())
+    pl.when(node > 0)(meet)
     weight_copy.wait()
     bias_copy.wait()
     column[...] = jnp.broadcast_to(bias[...], (block, bias.shape[1])).T
-    for step in range(1, nodes - 1):
-        for p in range(PIECES):
-            take(step - 1, p)
-            send(step, p)
-    pl.when(node > 1)(meet)
     for p in range(PIECES):
         own[p].wait()
         unpack_stripe(p, node)
     for step in range(nodes - 2):
-        for p in range(PIECES):
-            unpack(step, p)
+        for taken, stripe in ((takes_right(step), node - 1 - step), (takes_left(step), node + 1 + step)):
+            @pl.when(taken)
+            def _():
+                for p in range(PIECES):
+                    unpack_stripe(p, stripe)
+
     cols_copy.wait()
     tile_copy.wait()
     for p in range(PIECES):
@@ -187,16 +197,23 @@
     here = pl.ds(pl.multiple_of(feat * span, span), span)
     full[pl.ds(pl.multiple_of(feat * width, width), width), :] = agg[:, here]
 
+    for step in range(nodes - 1):
+        @pl.when(sends_right(step))
+        def _():
+            for p in range(PIECES):
+                right(step, p).wait_send()
+
+        @pl.when(sends_left(step))
+        def _():
+            for p in range(PIECES):
+                left(step, p).wait_send()
+
     total = jnp.concatenate([column[...]] * share, axis=1)
     for k in range(1, feats):
         exchange(k).wait_recv()
     total += jnp.dot(weight[...], full[...], preferred_element_type=jnp.float32)
     out[...] = total.astype(out.dtype)
 
-    for step in range(nodes - 1):
-        for p in range(PIECES):
-            pl.when(sends_right(step))(lambda: right(step, p).wait_send())
-            pl.when(sends_left(step))(lambda: left(step, p).wait_send())
     for k in range(1, feats):
         exchange(k).wait_send()
 

time: 22.7 us -> 22.4 us (0.987)
  Pallas kernels: 21.9 us -> 21.6 us
    pallas_call x1, Pallas kernels: 21.9 us -> 21.6 us  [on_device(): pl.pallas_call(functools.partial(kernel, nodes, feats), out_shape=pltpu.V...]
where the time goes in v3:
time: 22.4 us; the launch traced here: 22.2 us
  Pallas kernels  21.6 us (96%)
  local copies, waits for them, and re-layouts  0.66 us (3%)
    pallas_call x1, Pallas kernels, on_device(): pl.pallas_call(functools.partial(kernel, nodes, feats), out_shape=pltpu.V...  21.6 us
    unnamed x1, local copies, waits for them, and re-layouts  0.66 us

profile of v3, /device:TPU:0, one launch (start us, length us, event | category | flops | bytes accessed | tf_op | source)
XLA Modules:
  0.0 22.2 jit_solution(8462331935821345909)
XLA Ops:
  0.0 21.6 %shard_map.55 = bf16[172,384]{1,0:T(8,128)(2,1)S(1)} custom-call(s32[8,12]{1,0:T(8,128)} %bitcast.8, bf16[64,1536]{1,0:T(8,128)(2,1)} %bitcast.6, bf16[12,8,128,128]{3,2,1,0:T(8,128)(2,1)} %tiles_hbm.1, bf16[172,256]{1,0:T(8,128)(2,1)} %bitcast.7, f32[1,172]{1,0:T(1,128)} %bitcast.9), custom_call_target="tpu_custom_call" | custom-call | tf_op jit(solution)/shard_map/pallas_call | solution.py:227
  21.6 0.7 %copy.7 = bf16[384,172]{0,1:T(8,128)(2,1)} copy(bf16[384,172]{0,1:T(8,128)(2,1)S(1)} %bitcast.5) | data formatting | bytes 264192

commit v4 on v3

--- a/solution.py
+++ b/solution.py
@@ -9,7 +9,7 @@
 
 MESH = pl.DeviceIdType.MESH
 PIECES = 4
-LAG = 0
+EARLY = 2
 
 
 def kernel(nodes, feats, cols_hbm, x, tiles_hbm, weight_hbm, bias_hbm, out, cols, weight, bias, column, tiles, agg, full, blocks, own_sem, tile_sem, small_sem, right_send, right_recv, left_send, left_recv,
@@ -102,40 +102,57 @@
         pl.when(takes_right(step))(lambda: unpack_stripe(p, node - 1 - step))
         pl.when(takes_left(step))(lambda: unpack_stripe(p, node + 1 + step))
 
-    order = list(range(1, feats))
+    order, near = list(range(1, feats)), feats - 1
     if feats == 4:
-        order = [2 - odd, 3 - odd, 1 + 2 * odd]
-
-    def exchange(k):
+        order, near = [2 - odd, 3 - odd, 1 + 2 * odd], 3 - 2 * odd
+    split = EARLY * piece
+
+    def exchange(k, low, high):
         peer = lax.rem(feat + k, feats)
+        sem = 1 if low > 0 else 0
         return pltpu.make_async_remote_copy(
-            agg.at[:, pl.ds(pl.multiple_of(peer * span, span), span)],
-            full.at[pl.ds(pl.multiple_of(feat * width, width), width)],
-            ex_send.at[k], ex_recv.at[k], device_id={"feat": peer}, device_id_type=MESH,
+            agg.at[peer, pl.ds(low, high - low)],
+            full.at[pl.ds(pl.multiple_of(feat * width, width) + low, high - low)],
+            ex_send.at[k, sem], ex_recv.at[k, sem], device_id={"feat": peer}, device_id_type=MESH,
         )
 
-    def aggregate(i, carry):
-        k = jnp.int32(0)
-        for at, step in enumerate(order):
+    def pick(i, steps):
+        k = steps[0]
+        for at, step in enumerate(steps):
             k = jnp.where(i == at, step, k)
+        return k
+
+    def aggregate(k, low, high):
         peer = lax.rem(feat + k, feats)
         sums = []
         for j in range(share):
             r = peer * share + j
             sums.append(lax.dot_general(
-                jnp.concatenate([blocks[cols[s, r]] for s in range(slots)], axis=1),
+                jnp.concatenate([blocks[cols[s, r], low:high, :] for s in range(slots)], axis=1),
                 jnp.concatenate([tiles[r, s] for s in range(slots)], axis=1),
                 (((1,), (1,)), ((), ())),
                 preferred_element_type=jnp.float32,
             ))
-        rounded = jnp.concatenate(sums, axis=1).astype(jnp.bfloat16)
-        agg[:, pl.ds(pl.multiple_of(peer * span, span), span)] = rounded
-
-        @pl.when(i < feats - 1)
-        def _():
-            exchange(k).start()
-
-        return carry
+        agg[peer, low:high] = jnp.concatenate(sums, axis=1).astype(jnp.bfloat16)
+
+    def far_peers(low, high):
+        def turn(i, carry):
+            k = pick(i, order[:-1])
+            aggregate(k, low, high)
+            exchange(k, low, high).start()
+            return carry
+
+        if feats > 2:
+            lax.fori_loop(0, feats - 2, turn, 0)
+
+    def near_peers():
+        def turn(i, carry):
+            k = pick(i, [order[-1], 0])
+            aggregate(k, 0, width)
+            pl.when(i == 0)(lambda: exchange(k, 0, width).start())
+            return carry
+
+        lax.fori_loop(0, 2, turn, 0)
 
     @pl.when(sends_left(0))
     def _():
@@ -162,16 +179,17 @@
     tile_copy.start()
 
     pl.when(node == 0)(meet)
-    turns = [(step, p) for step in range(1, nodes - 1) for p in range(PIECES)]
-    for at in range(len(turns) + LAG):
-        if at < len(turns):
-            step, p = turns[at]
-            pl.when(takes_left(step - 1))(lambda: left(step - 1, p).wait_recv())
-            pl.when(sends_left(step))(lambda: left(step, p).start())
-        if at >= LAG:
-            step, p = turns[at - LAG]
-            pl.when(takes_right(step - 1))(lambda: right(step - 1, p).wait_recv())
-            pl.when(sends_right(step))(lambda: right(step, p).start())
+    for step in range(1, nodes - 1):
+        for p in range(PIECES):
+            @pl.when(sends_left(step))
+            def _():
+                left(step - 1, p).wait_recv()
+                left(step, p).start()
+
+            @pl.when(sends_right(step))
+            def _():
+                right(step - 1, p).wait_recv()
+                right(step, p).start()
     pl.when(node > 0)(meet)
     weight_copy.wait()
     bias_copy.wait()
@@ -180,22 +198,31 @@
         own[p].wait()
         unpack_stripe(p, node)
     for step in range(nodes - 2):
-        for taken, stripe in ((takes_right(step), node - 1 - step), (takes_left(step), node + 1 + step)):
-            @pl.when(taken)
-            def _():
-                for p in range(PIECES):
-                    unpack_stripe(p, stripe)
+        @pl.when(takes_right(step))
+        def _():
+            for p in range(PIECES):
+                pl.when(jnp.logical_not(sends_right(step + 1)))(lambda: right(step, p).wait_recv())
+                unpack_stripe(p, node - 1 - step)
+
+        @pl.when(takes_left(step))
+        def _():
+            for p in range(PIECES):
+                pl.when(jnp.logical_not(sends_left(step + 1)))(lambda: left(step, p).wait_recv())
+                unpack_stripe(p, node + 1 + step)
 
     cols_copy.wait()
     tile_copy.wait()
-    for p in range(PIECES):
+    for p in range(EARLY):
         take(nodes - 2, p)
         unpack(nodes - 2, p)
-
-    lax.fori_loop(0, feats, aggregate, 0)
-
-    here = pl.ds(pl.multiple_of(feat * span, span), span)
-    full[pl.ds(pl.multiple_of(feat * width, width), width), :] = agg[:, here]
+    far_peers(0, split)
+    for p in range(EARLY, PIECES):
+        take(nodes - 2, p)
+        unpack(nodes - 2, p)
+    far_peers(split, width)
+    near_peers()
+
+    full[pl.ds(pl.multiple_of(feat * width, width), width), :] = agg[feat]
 
     for step in range(nodes - 1):
         @pl.when(sends_right(step))
@@ -210,12 +237,27 @@
 
     total = jnp.concatenate([column[...]] * share, axis=1)
     for k in range(1, feats):
-        exchange(k).wait_recv()
+        @pl.when(k == near)
+        def _():
+            exchange(k, 0, width).wait_recv()
+
+        @pl.when(k != near)
+        def _():
+            exchange(k, 0, split).wait_recv()
+            exchange(k, split, width).wait_recv()
+
     total += jnp.dot(weight[...], full[...], preferred_element_type=jnp.float32)
     out[...] = total.astype(out.dtype)
 
     for k in range(1, feats):
-        exchange(k).wait_send()
+        @pl.when(k == order[-1])
+        def _():
+            exchange(k, 0, width).wait_send()
+
+        @pl.when(k != order[-1])
+        def _():
+            exchange(k, 0, split).wait_send()
+            exchange(k, split, width).wait_send()
 
 
 def on_device(nodes, feats, features, tiles, col_block, weight, bias):
@@ -241,7 +283,7 @@
             pltpu.VMEM((1, classes), bias.dtype),
             pltpu.VMEM((classes, block), bias.dtype),
             pltpu.VMEM(tiles.shape, tiles.dtype),
-            pltpu.VMEM((width, rows), features.dtype),
+            pltpu.VMEM((feats, width, share), features.dtype),
             pltpu.VMEM((feats * width, share), features.dtype),
             pltpu.VMEM((nodes * block_rows, width, block), features.dtype),
             pltpu.SemaphoreType.DMA((PIECES,)),
@@ -251,8 +293,8 @@
             pltpu.SemaphoreType.DMA((nodes - 1, PIECES)),
             pltpu.SemaphoreType.DMA((nodes - 1, PIECES)),
             pltpu.SemaphoreType.DMA((nodes - 1, PIECES)),
-            pltpu.SemaphoreType.DMA((feats,)),
-            pltpu.SemaphoreType.DMA((feats,)),
+            pltpu.SemaphoreType.DMA((feats, 2)),
+            pltpu.SemaphoreType.DMA((feats, 2)),
             pltpu.SemaphoreType.REGULAR,
             pltpu.SemaphoreType.REGULAR,
             pltpu.SemaphoreType.REGULAR,

time: 22.4 us -> 22.2 us (level)
  no operation moved by 1% of the time
where the time goes in v4:
time: 22.2 us; the launch traced here: 22 us
  Pallas kernels  21.4 us (96%)
  local copies, waits for them, and re-layouts  0.66 us (3%)
    pallas_call x1, Pallas kernels, on_device(): pl.pallas_call(functools.partial(kernel, nodes, feats), out_shape=pltpu.V...  21.4 us
    unnamed x1, local copies, waits for them, and re-layouts  0.66 us

profile of v4, /device:TPU:0, one launch (start us, length us, event | category | flops | bytes accessed | tf_op | source)
XLA Modules:
  0.0 22.0 jit_solution(6088622853791763796)
XLA Ops:
  0.0 21.4 %shard_map.55 = bf16[172,384]{1,0:T(8,128)(2,1)S(1)} custom-call(s32[8,12]{1,0:T(8,128)} %bitcast.8, bf16[64,1536]{1,0:T(8,128)(2,1)} %bitcast.6, bf16[12,8,128,128]{3,2,1,0:T(8,128)(2,1)} %tiles_hbm.1, bf16[172,256]{1,0:T(8,128)(2,1)} %bitcast.7, f32[1,172]{1,0:T(1,128)} %bitcast.9), custom_call_target="tpu_custom_call" | custom-call | tf_op jit(solution)/shard_map/pallas_call | solution.py:269
  21.4 0.7 %copy.7 = bf16[384,172]{0,1:T(8,128)(2,1)} copy(bf16[384,172]{0,1:T(8,128)(2,1)S(1)} %bitcast.5) | data formatting | bytes 264192

commit v5 on v4

--- a/solution.py
+++ b/solution.py
@@ -96,7 +96,7 @@
             blocks[stripe * block_rows + b, p * piece:(p + 1) * piece, :] = held[p][:, pl.ds(at, block)]
             return carry
 
-        lax.fori_loop(0, block_rows, one, 0, unroll=False)
+        lax.fori_loop(0, block_rows, one, 0, unroll=nodes <= 8)
 
     def unpack(step, p):
         pl.when(takes_right(step))(lambda: unpack_stripe(p, node - 1 - step))

time: 22.2 us -> 22.1 us (level)
  no operation moved by 1% of the time
where the time goes in v5:
time: 22.1 us; the launch traced here: 22 us
  Pallas kernels  21.3 us (96%)
  local copies, waits for them, and re-layouts  0.66 us (3%)
    pallas_call x1, Pallas kernels, on_device(): pl.pallas_call(functools.partial(kernel, nodes, feats), out_shape=pltpu.V...  21.3 us
    unnamed x1, local copies, waits for them, and re-layouts  0.66 us

profile of v5, /device:TPU:0, one launch (start us, length us, event | category | flops | bytes accessed | tf_op | source)
XLA Modules:
  0.0 22.0 jit_solution(14052092292789739116)
XLA Ops:
  0.0 21.3 %shard_map.55 = bf16[172,384]{1,0:T(8,128)(2,1)S(1)} custom-call(s32[8,12]{1,0:T(8,128)} %bitcast.8, bf16[64,1536]{1,0:T(8,128)(2,1)} %bitcast.6, bf16[12,8,128,128]{3,2,1,0:T(8,128)(2,1)} %tiles_hbm.1, bf16[172,256]{1,0:T(8,128)(2,1)} %bitcast.7, f32[1,172]{1,0:T(1,128)} %bitcast.9), custom_call_target="tpu_custom_call" | custom-call | tf_op jit(solution)/shard_map/pallas_call | solution.py:269
  21.3 0.7 %copy.7 = bf16[384,172]{0,1:T(8,128)(2,1)} copy(bf16[384,172]{0,1:T(8,128)(2,1)S(1)} %bitcast.5) | data formatting | bytes 264192

commit v6 on v5

--- a/solution.py
+++ b/solution.py
@@ -13,7 +13,7 @@
 
 
 def kernel(nodes, feats, cols_hbm, x, tiles_hbm, weight_hbm, bias_hbm, out, cols, weight, bias, column, tiles, agg, full, blocks, own_sem, tile_sem, small_sem, right_send, right_recv, left_send, left_recv,
-           ex_send, ex_recv, right_in, above_in, feats_in, *held):
+           ex_send, ex_recv, right_in, above_in, feats_in, partial, *held):
     node = lax.axis_index("node")
     feat = lax.axis_index("feat")
     odd = lax.rem(feat, 2)
@@ -236,17 +236,26 @@
                 left(step, p).wait_send()
 
     total = jnp.concatenate([column[...]] * share, axis=1)
+    left_over = slice(None)
+    if feats == 4:
+        exchange(near, 0, width).wait_recv()
+        chip = pl.ds(pl.multiple_of((feat - odd) * width, 2 * width), 2 * width)
+        left_over = pl.ds(pl.multiple_of((2 - feat + odd) * width, 2 * width), 2 * width)
+        partial[...] = total + jnp.dot(weight[:, chip], full[chip, :], preferred_element_type=jnp.float32)
     for k in range(1, feats):
-        @pl.when(k == near)
-        def _():
-            exchange(k, 0, width).wait_recv()
+        if feats != 4:
+            @pl.when(k == near)
+            def _():
+                exchange(k, 0, width).wait_recv()
 
         @pl.when(k != near)
         def _():
             exchange(k, 0, split).wait_recv()
             exchange(k, split, width).wait_recv()
 
-    total += jnp.dot(weight[...], full[...], preferred_element_type=jnp.float32)
+    if feats == 4:
+        total = partial[...]
+    total += jnp.dot(weight[:, left_over], full[left_over, :], preferred_element_type=jnp.float32)
     out[...] = total.astype(out.dtype)
 
     for k in range(1, feats):
@@ -298,6 +307,7 @@
             pltpu.SemaphoreType.REGULAR,
             pltpu.SemaphoreType.REGULAR,
             pltpu.SemaphoreType.REGULAR,
+            pltpu.VMEM((classes, share), jnp.float32),
             *[pltpu.VMEM((piece, nodes * rows), features.dtype)] * PIECES,
         ],
         compiler_params=pltpu.CompilerParams(collective_id=0, has_side_effects=True),

time: 22.1 us -> 22.1 us (level)
  no operation moved by 1% of the time
where the time goes in v6:
time: 22.1 us; the launch traced here: 22 us
  Pallas kernels  21.3 us (96%)
  local copies, waits for them, and re-layouts  0.66 us (3%)
    pallas_call x1, Pallas kernels, on_device(): pl.pallas_call(functools.partial(kernel, nodes, feats), out_shape=pltpu.V...  21.3 us
    unnamed x1, local copies, waits for them, and re-layouts  0.66 us

profile of v6, /device:TPU:0, one launch (start us, length us, event | category | flops | bytes accessed | tf_op | source)
XLA Modules:
  0.0 22.0 jit_solution(4795943294486154259)
XLA Ops:
  0.0 21.3 %shard_map.55 = bf16[172,384]{1,0:T(8,128)(2,1)S(1)} custom-call(s32[8,12]{1,0:T(8,128)} %bitcast.8, bf16[64,1536]{1,0:T(8,128)(2,1)} %bitcast.6, bf16[12,8,128,128]{3,2,1,0:T(8,128)(2,1)} %tiles_hbm.1, bf16[172,256]{1,0:T(8,128)(2,1)} %bitcast.7, f32[1,172]{1,0:T(1,128)} %bitcast.9), custom_call_target="tpu_custom_call" | custom-call | tf_op jit(solution)/shard_map/pallas_call | solution.py:278
  21.3 0.7 %copy.7 = bf16[384,172]{0,1:T(8,128)(2,1)} copy(bf16[384,172]{0,1:T(8,128)(2,1)S(1)} %bitcast.5) | data formatting | bytes 264192

commit v7 on v5

--- a/solution.py
+++ b/solution.py
@@ -36,6 +36,15 @@
         for peer in peers:
             pl.semaphore_signal(barrier, inc=1, device_id={"feat": peer}, device_id_type=MESH)
 
+    weight_copy = pltpu.make_async_copy(weight_hbm, weight, small_sem.at[1])
+    weight_copy.start()
+    bias_copy = pltpu.make_async_copy(bias_hbm, bias, small_sem.at[2])
+    bias_copy.start()
+    cols_copy = pltpu.make_async_copy(cols_hbm, cols, small_sem.at[0])
+    cols_copy.start()
+    tile_copy = pltpu.make_async_copy(tiles_hbm, tiles, tile_sem)
+    tile_copy.start()
+
     pl.semaphore_wait(barrier, jnp.where(node == 0, feats - 1, 1))
 
     @pl.when(node > 0)
@@ -169,15 +178,6 @@
     own = [pltpu.make_async_copy(source(0, p, node), stripe_of(p, node), own_sem.at[p]) for p in range(PIECES)]
     for copy in own:
         copy.start()
-    weight_copy = pltpu.make_async_copy(weight_hbm, weight, small_sem.at[1])
-    weight_copy.start()
-    bias_copy = pltpu.make_async_copy(bias_hbm, bias, small_sem.at[2])
-    bias_copy.start()
-    cols_copy = pltpu.make_async_copy(cols_hbm, cols, small_sem.at[0])
-    cols_copy.start()
-    tile_copy = pltpu.make_async_copy(tiles_hbm, tiles, tile_sem)
-    tile_copy.start()
-
     pl.when(node == 0)(meet)
     for step in range(1, nodes - 1):
         for p in range(PIECES):

time: 22.1 us -> 22.1 us (level)
  no operation moved by 1% of the time
where the time goes in v7:
time: 22.1 us; the launch traced here: 22 us
  Pallas kernels  21.3 us (96%)
  local copies, waits for them, and re-layouts  0.66 us (3%)
    pallas_call x1, Pallas kernels, on_device(): pl.pallas_call(functools.partial(kernel, nodes, feats), out_shape=pltpu.V...  21.3 us
    unnamed x1, local copies, waits for them, and re-layouts  0.66 us

profile of v7, /device:TPU:0, one launch (start us, length us, event | category | flops | bytes accessed | tf_op | source)
XLA Modules:
  0.0 22.0 jit_solution(7554744633293402958)
XLA Ops:
  0.0 21.3 %shard_map.55 = bf16[172,384]{1,0:T(8,128)(2,1)S(1)} custom-call(s32[8,12]{1,0:T(8,128)} %bitcast.8, bf16[64,1536]{1,0:T(8,128)(2,1)} %bitcast.6, bf16[12,8,128,128]{3,2,1,0:T(8,128)(2,1)} %tiles_hbm.1, bf16[172,256]{1,0:T(8,128)(2,1)} %bitcast.7, f32[1,172]{1,0:T(1,128)} %bitcast.9), custom_call_target="tpu_custom_call" | custom-call | tf_op jit(solution)/shard_map/pallas_call | solution.py:269
  21.3 0.7 %copy.7 = bf16[384,172]{0,1:T(8,128)(2,1)} copy(bf16[384,172]{0,1:T(8,128)(2,1)S(1)} %bitcast.5) | data formatting | bytes 264192
